TPU v7x, 512 devices: a whole 4x8x8 slice. The times are simulated.
512 devices in a mesh: dp: 4 (over x), expert: 128 (over z, y, core).
Axes of the slice: x: 4, y: 8, z: 8, core: 2. Of those that a mesh axis runs over, the one named last changes fastest.
Arguments:
- tokens: bfloat16 [8192, 2048], P(('dp', 'expert')), may hold values from -6 to 6
- cotangent: bfloat16 [8192, 2048], P(('dp', 'expert')), may hold values from -6 to 6
- routes: int32 [8192, 8], P(('dp', 'expert')), may hold values from 0 to 127, all different within a row; in each aligned block of 16 rows (0 to 15, 16 to 31, ...) at most 2 rows name the same one
- gate_values: float32 [8192, 8], P(('dp', 'expert')), may hold values from 0.1 to 1
- gate_weight: bfloat16 [128, 768, 2048], P('expert', 'dp'), may hold values from -0.125 to 0.125
- up_weight: bfloat16 [128, 768, 2048], P('expert', 'dp'), may hold values from -0.125 to 0.125
- down_weight: bfloat16 [128, 768, 2048], P('expert', None, 'dp'), may hold values from -0.21875 to 0.21875
Outputs:
- mixed: bfloat16 [8192, 2048], P(('dp', 'expert'))
- grad_gate_weight: bfloat16 [128, 768, 2048], P('expert', 'dp')
- grad_up_weight: bfloat16 [128, 768, 2048], P('expert', 'dp')
- grad_down_weight: bfloat16 [128, 768, 2048], P('expert', None, 'dp')
Inputs may be any that keep to these rules, and one draw needn't show every extreme that they name: `routes`: each row names 8 different experts. Among the rows of one device no expert is named more than 2 times, and in some device's rows some expert is named exactly 2 times.
All inputs are finite; a program needn't handle non-finite values.
Results may differ from a plain program's by a relative error of at most 0.0058.
Values may be sent and summed in bfloat16 or wider, within the bound.
A program may use at most 64 MiB of HBM per device.

v0:
```python
import jax
import jax.numpy as jnp
from jax import lax
from jax.sharding import PartitionSpec as P


def body(tokens, cotangent, routes, gate_values, gate_weight, up_weight, down_weight):
    tok_rows = tokens.shape[0]
    width = tokens.shape[1]
    top_count = routes.shape[1]
    experts = lax.axis_size("expert")
    groups = lax.axis_size("dp")
    capacity = min(tok_rows, max(2, 2 * tok_rows * top_count // experts))
    onehot = routes[:, :, None] == jnp.arange(experts, dtype=jnp.int32)[None, None, :]
    named = jnp.sum(onehot.astype(jnp.int32), axis=1)
    earlier = jnp.cumsum(named, axis=0) - named
    slot_ids = jnp.arange(capacity, dtype=jnp.int32)[None, :, None]
    placer = (named.T[:, None, :] == 1) & (earlier.T[:, None, :] == slot_ids)
    placer_half = placer.astype(jnp.bfloat16)
    placer_full = placer.astype(jnp.float32)
    token_gate = jnp.sum(
        jnp.where(onehot, gate_values[:, :, None], jnp.zeros((), jnp.float32)), axis=1
    )
    slot_gate = jnp.sum(placer_full * token_gate.T[:, None, :], axis=2)
    row_input = jnp.einsum(
        "est,td->esd", placer_half, tokens, preferred_element_type=jnp.float32
    ).astype(jnp.bfloat16)
    picked_cot = jnp.einsum(
        "est,td->esd", placer_half, cotangent, preferred_element_type=jnp.float32
    )
    row_cot = (slot_gate[:, :, None] * picked_cot).astype(jnp.bfloat16)
    arrived_input, arrived_cot = (
        lax.all_to_all(row_input, "expert", split_axis=0, concat_axis=0, tiled=True),
        lax.all_to_all(row_cot, "expert", split_axis=0, concat_axis=0, tiled=True),
    )
    local_rows = arrived_input.shape[0] * arrived_input.shape[1]
    flat_input = arrived_input.reshape(local_rows, width)
    flat_cot = arrived_cot.reshape(local_rows, width)
    gate_local = gate_weight[0]
    up_local = up_weight[0]
    down_local = down_weight[0]
    quarter_width = down_local.shape[1]
    inputs_all = lax.all_gather(flat_input, "dp", axis=0, tiled=True)
    cot_quarter = lax.all_to_all(flat_cot, "dp", split_axis=1, concat_axis=0, tiled=True)
    contract_last = (((1,), (1,)), ((), ()))
    gate_pre = lax.dot_general(
        gate_local, inputs_all, contract_last, preferred_element_type=jnp.float32
    )
    up_pre = lax.dot_general(
        up_local, inputs_all, contract_last, preferred_element_type=jnp.float32
    )
    hidden_part = (jax.nn.silu(gate_pre) * up_pre).astype(jnp.bfloat16)
    hidden_all = lax.all_gather(hidden_part, "dp", axis=0, tiled=True)
    contract_lead = (((0,), (0,)), ((), ()))
    expert_out = lax.dot_general(
        hidden_all, down_local, contract_lead, preferred_element_type=jnp.float32
    ).astype(jnp.bfloat16)
    grad_down = jnp.dot(hidden_all, cot_quarter, preferred_element_type=jnp.float32).astype(
        jnp.bfloat16
    )
    grad_hidden = lax.psum_scatter(
        lax.dot_general(down_local, cot_quarter, contract_last, preferred_element_type=jnp.float32),
        "dp",
        scatter_dimension=0,
        tiled=True,
    )
    sigma = jax.nn.sigmoid(gate_pre)
    grad_gate = (grad_hidden * up_pre * sigma * (1.0 + gate_pre * (1.0 - sigma))).astype(
        jnp.bfloat16
    )
    grad_up = (grad_hidden * jax.nn.silu(gate_pre)).astype(jnp.bfloat16)
    grad_gate_local = jnp.dot(grad_gate, inputs_all, preferred_element_type=jnp.float32).astype(
        jnp.bfloat16
    )
    grad_up_local = jnp.dot(grad_up, inputs_all, preferred_element_type=jnp.float32).astype(
        jnp.bfloat16
    )
    out_blocks = expert_out.reshape(groups, experts, capacity, quarter_width)
    returned = lax.all_to_all(
        lax.all_to_all(out_blocks, "dp", split_axis=0, concat_axis=3, tiled=True),
        "expert",
        split_axis=1,
        concat_axis=1,
        tiled=True,
    )
    returned_rows = returned.reshape(experts * capacity, width).astype(jnp.float32)
    combine_rows = (placer_full * slot_gate[:, :, None]).reshape(experts * capacity, tok_rows)
    mixed = lax.dot_general(
        combine_rows,
        returned_rows,
        contract_lead,
        precision=lax.Precision.HIGHEST,
        preferred_element_type=jnp.float32,
    ).astype(jnp.bfloat16)
    return (mixed, grad_gate_local[None], grad_up_local[None], grad_down[None])


def solution(mesh):
    in_specs = (
        P(("dp", "expert"), None),
        P(("dp", "expert"), None),
        P(("dp", "expert"), None),
        P(("dp", "expert"), None),
        P("expert", "dp", None),
        P("expert", "dp", None),
        P("expert", None, "dp"),
    )
    out_specs = (
        P(("dp", "expert"), None),
        P("expert", "dp", None),
        P("expert", "dp", None),
        P("expert", None, "dp"),
    )
    return jax.shard_map(body, mesh=mesh, in_specs=in_specs, out_specs=out_specs, check_vma=False)
```

profile of v0, /device:TPU:1, one launch (start us, length us, event | category | flops | bytes accessed | tf_op | source)
XLA Modules:
  0.0 236.6 jit_solution(17935731720747272963)
XLA Ops:
  7.2 0.0 copy-start
  7.2 0.0 all-gather.3.cloned.1.call-start
  7.2 0.8 copy.53
  8.0 0.1 convert_reduce_fusion
  8.2 0.8 copy.56
  9.0 0.1 select_reduce_fusion.1
  9.1 0.1 copy.54
  9.2 0.1 copy.57
  9.3 0.1 copy.55
  9.4 0.3 select_reduce_fusion
  9.7 0.1 copy.58
  9.8 1.3 convolution_convert_fusion
  11.1 1.1 copy.59
  12.2 49.3 %all_to_all.52 = bf16[128,2,2048]{2,1,0:T(2,128)(2,1)S(1)} all-to-all(bf16[128,2,2048]{2,1,0:T(2,128)(2,1)S(1)} %copy.59), channel_id=1, replica_groups=mesh['dp'=4,'expert'=128] {'expert'}, dimensions={0} | all-to-all | bytes 2097152 | tf_op jit(solution)/shard_map/all_to_all | solution.py:33
  61.4 1.2 reshape.91
  62.6 0.0 all-gather.3.cloned.1.call-update
  62.7 0.1 copy.63
  62.7 0.5 fusion
  63.2 2.1 copy.65
  65.3 6.5 %all-to-all-start.3 = ((bf16[128,2,2048]{2,1,0:T(2,128)(2,1)}), bf16[128,2,2048]{2,1,0:T(2,128)(2,1)S(1)}, u32[]{:S(2)}, u32[]{:S(2)}) async-start(bf16[128,2,2048]{2,1,0:T(2,128)(2,1)} %copy.65), calls=%async_computation.3 | async-start | bytes 2097152 | tf_op jit(solution)/shard_map/all_to_all | solution.py:34
  71.8 0.0 all-gather.5.cloned.1.call-start
  71.8 38.1 %all-gather.3.cloned.1.call-done = bf16[1024,2048]{1,0:T(8,128)(2,1)} async-done(((bf16[256,2048]{1,0:T(8,128)(2,1)}), bf16[1024,2048]{1,0:T(8,128)(2,1)}) %all-gather.3.cloned.1.call-update) | async-done | bytes 4194320 | tf_op jit(solution)/shard_map/all_gather | solution.py:43
  110.0 3.9 %convolution_bitcast_fusion.2 = f32[192,1024]{1,0:T(8,128)S(1)} fusion(bf16[1024,2048]{1,0:T(8,128)(2,1)} %all-gather.3.cloned.1.call-done, bf16[1,192,2048]{2,1,0:T(8,128)(2,1)S(1)} %copy-done.5), kind=kOutput, calls=%fused_computation.13 | convolution fusion | flops 805306368 | bytes 5767168 | tf_op jit(solution)/shard_map/dot_general | solution.py:46
  113.8 0.0 copy-start.8
  113.9 2.6 %multiply_convert_fusion.2 = (bf16[192,1024]{1,0:T(8,128)(2,1)}, f32[192,1024]{1,0:T(8,128)}) fusion(f32[192,1024]{1,0:T(8,128)S(1)} %convolution_bitcast_fusion.2, bf16[1024,2048]{1,0:T(8,128)(2,1)S(1)} %copy-done.2, bf16[1,192,2048]{2,1,0:T(8,128)(2,1)S(1)} %copy-done.6), kind=kOutput, calls=%fused_computation.20 | convolution fusion | flops 806486016 | bytes 6946816 | tf_op jit(solution)/shard_map/dot_general | solution.py:49
  116.5 0.0 all-gather.5.cloned.1.call-update
  116.5 0.0 reduce-scatter.2.cloned.1.call-start
  116.6 0.7 all_to_all.43
  117.3 0.2 copy.66
  117.5 17.0 %all_to_all.53 = bf16[256,4,512]{2,0,1:T(8,128)(2,1)S(1)} all-to-all(bf16[256,4,512]{2,0,1:T(8,128)(2,1)S(1)} %copy.66), channel_id=1, replica_groups=mesh['dp'=4,'expert'=128] {'dp'}, dimensions={1} | all-to-all | bytes 2097152 | tf_op jit(solution)/shard_map/all_to_all | solution.py:44
  134.5 2.7 %convolution_bitcast_fusion = f32[768,1024]{1,0:T(8,128)} fusion(bf16[1024,512]{1,0:T(8,128)(2,1)S(1)} %bitcast.59, bf16[1,768,512]{2,1,0:T(8,128)(2,1)S(1)} %copy-done), kind=kOutput, calls=%fused_computation.8 | convolution fusion | flops 805306368 | bytes 4980736 | tf_op jit(solution)/shard_map/dot_general | solution.py:62
  137.2 0.0 reduce-scatter.2.cloned.1.call-update
  137.3 11.7 %all-gather.5.cloned.1.call-done = bf16[768,1024]{1,0:T(8,128)(2,1)} async-done(((bf16[192,1024]{1,0:T(8,128)(2,1)}), bf16[768,1024]{1,0:T(8,128)(2,1)}) %all-gather.5.cloned.1.call-update) | async-done | bytes 1572880 | tf_op jit(solution)/shard_map/all_gather | solution.py:53
  148.9 3.4 %convolution_convert_fusion.4 = bf16[1024,512]{1,0:T(8,128)(2,1)} fusion(bf16[768,1024]{1,0:T(8,128)(2,1)} %all-gather.5.cloned.1.call-done, bf16[1,768,512]{2,1,0:T(8,128)(2,1)S(1)} %copy-done), kind=kOutput, calls=%fused_computation.9 | convolution fusion | flops 805830656 | bytes 3407872 | tf_op jit(solution)/shard_map/dot_general | solution.py:55
  152.3 1.5 reshape.92
  153.8 2.0 copy.60
  155.8 21.9 %all_to_all.54 = bf16[4,128,2,512]{1,3,2,0:T(8,128)(2,1)S(1)} all-to-all(bf16[4,128,2,512]{1,3,2,0:T(8,128)(2,1)} %copy.60), channel_id=1, replica_groups=mesh['dp'=4,'expert'=128] {'dp'}, dimensions={0} | all-to-all | bytes 2097152 | tf_op jit(solution)/shard_map/all_to_all | solution.py:80
  177.7 0.1 copy.61
  177.7 2.1 copy.62
  179.8 17.7 %all-to-all-start.2 = ((bf16[1,128,2,2048]{3,2,0,1:T(2,128)(2,1)}), bf16[1,128,2,2048]{3,2,0,1:T(2,128)(2,1)S(1)}, u32[]{:S(2)}, u32[]{:S(2)}) async-start(bf16[1,128,2,2048]{3,2,0,1:T(2,128)(2,1)} %copy.62), calls=%async_computation.2 | async-start | bytes 2097152 | tf_op jit(solution)/shard_map/all_to_all | solution.py:79
  197.5 0.2 broadcast_select_fusion
  197.7 3.4 %reduce-scatter.2.cloned.1.call-done = f32[192,1024]{1,0:T(8,128)} async-done(((f32[768,1024]{1,0:T(8,128)}), f32[192,1024]{1,0:T(8,128)}) %reduce-scatter.2.cloned.1.call-update) | async-done | bytes 786448 | tf_op jit(solution)/shard_map/reduce_scatter | solution.py:61
  201.2 4.7 %fusion.2 = bf16[1,192,2048]{2,1,0:T(8,128)(2,1)} fusion(bf16[1024,2048]{1,0:T(8,128)(2,1)} %all-gather.3.cloned.1.call-done, f32[192,1024]{1,0:T(8,128)} %reduce-scatter.2.cloned.1.call-done, f32[192,1024]{1,0:T(8,128)} %copy-done.8), kind=kOutput, calls=%fused_computation.6 | convolution fusion | flops 806879232 | bytes 6553600 | tf_op jit(solution)/shard_map/dot_general | solution.py:75
  205.9 2.0 fusion.1
  208.0 1.9 fusion.3
  209.8 18.6 %all-to-all-done.2 = bf16[1,128,2,2048]{3,2,0,1:T(2,128)(2,1)S(1)} async-done(((bf16[1,128,2,2048]{3,2,0,1:T(2,128)(2,1)}), bf16[1,128,2,2048]{3,2,0,1:T(2,128)(2,1)S(1)}, u32[]{:S(2)}, u32[]{:S(2)}) %all-to-all-start.2) | async-done | bytes 1048608 | tf_op jit(solution)/shard_map/all_to_all | solution.py:79
  228.4 0.4 reshape.93
  228.9 1.2 convolution_convert_fusion.3
  (24 shorter events, 0.1 us)
Async XLA Ops:
  7.2 127.4 %copy-start = (bf16[1,768,512]{2,1,0:T(8,128)(2,1)S(1)}, bf16[1,768,512]{2,1,0:T(8,128)(2,1)}, u32[]{:S(2)}) copy-start(bf16[1,768,512]{2,1,0:T(8,128)(2,1)} %param.13) | copy-start | bytes 2359300
  7.2 102.8 %all-gather.3.cloned.1.call-start = ((), (), s32[]{:S(2)}) async-start(), calls=%async_computation.6 | async-start | bytes 5242880 | tf_op jit(solution)/shard_map/all_gather | solution.py:43
  12.2 50.6 %copy-start.1 = (bf16[16,2048]{1,0:T(8,128)(2,1)S(1)}, bf16[16,2048]{1,0:T(8,128)(2,1)}, u32[]{:S(2)}) copy-start(bf16[16,2048]{1,0:T(8,128)(2,1)} %param.8) | copy-start | bytes 196612
  62.6 47.3 %copy-start.5 = (bf16[1,192,2048]{2,1,0:T(8,128)(2,1)S(1)}, bf16[1,192,2048]{2,1,0:T(8,128)(2,1)}, u32[]{:S(2)}) copy-start(bf16[1,192,2048]{2,1,0:T(8,128)(2,1)} %param.11) | copy-start | bytes 2359300
  65.3 51.3 %all-to-all-start.3 = ((bf16[128,2,2048]{2,1,0:T(2,128)(2,1)}), bf16[128,2,2048]{2,1,0:T(2,128)(2,1)S(1)}, u32[]{:S(2)}, u32[]{:S(2)}) async-start(bf16[128,2,2048]{2,1,0:T(2,128)(2,1)} %copy.65), calls=%async_computation.3 | async-start | bytes 2097152 | tf_op jit(solution)/shard_map/all_to_all | solution.py:34
  71.8 42.0 %copy-start.6 = (bf16[1,192,2048]{2,1,0:T(8,128)(2,1)S(1)}, bf16[1,192,2048]{2,1,0:T(8,128)(2,1)}, u32[]{:S(2)}) copy-start(bf16[1,192,2048]{2,1,0:T(8,128)(2,1)} %param.12) | copy-start | bytes 2359300
  71.8 77.1 %all-gather.5.cloned.1.call-start = ((), (), s32[]{:S(2)}) async-start(), calls=%async_computation.7 | async-start | bytes 1966080 | tf_op jit(solution)/shard_map/all_gather | solution.py:53
  110.0 3.9 %copy-start.2 = (bf16[1024,2048]{1,0:T(8,128)(2,1)S(1)}, bf16[1024,2048]{1,0:T(8,128)(2,1)}, u32[]{:S(2)}) copy-start(bf16[1024,2048]{1,0:T(8,128)(2,1)} %all-gather.3.cloned.1.call-done) | copy-start | bytes 12582916
  113.8 2.6 %copy-start.8 = (f32[192,1024]{1,0:T(8,128)}, f32[192,1024]{1,0:T(8,128)S(1)}, u32[]{:S(2)}) copy-start(f32[192,1024]{1,0:T(8,128)S(1)} %convolution_bitcast_fusion.2) | copy-start | bytes 2359300
  116.5 84.6 %reduce-scatter.2.cloned.1.call-start = ((), (), s32[]{:S(2)}) async-start(), calls=%async_computation.8 | async-start | bytes 3932160 | tf_op jit(solution)/shard_map/reduce_scatter | solution.py:61
  179.8 48.6 %all-to-all-start.2 = ((bf16[1,128,2,2048]{3,2,0,1:T(2,128)(2,1)}), bf16[1,128,2,2048]{3,2,0,1:T(2,128)(2,1)S(1)}, u32[]{:S(2)}, u32[]{:S(2)}) async-start(bf16[1,128,2,2048]{3,2,0,1:T(2,128)(2,1)} %copy.62), calls=%async_computation.2 | async-start | bytes 2097152 | tf_op jit(solution)/shard_map/all_to_all | solution.py:79
  201.2 4.7 %copy-start.3 = (bf16[1024,2048]{1,0:T(8,128)(2,1)S(1)}, bf16[1024,2048]{1,0:T(8,128)(2,1)}, u32[]{:S(2)}) copy-start(bf16[1024,2048]{1,0:T(8,128)(2,1)} %all-gather.3.cloned.1.call-done) | copy-start | bytes 12582916
  201.2 4.7 %copy-start.7 = (f32[192,1024]{1,0:T(8,128)S(1)}, f32[192,1024]{1,0:T(8,128)}, u32[]{:S(2)}) copy-start(f32[192,1024]{1,0:T(8,128)} %reduce-scatter.2.cloned.1.call-done) | copy-start | bytes 2359300
  201.2 4.7 %copy-start.9 = (f32[192,1024]{1,0:T(8,128)S(1)}, f32[192,1024]{1,0:T(8,128)}, u32[]{:S(2)}) copy-start(f32[192,1024]{1,0:T(8,128)} %copy-done.8) | copy-start | bytes 2359300
  201.2 4.7 %copy-start.10 = (f32[192,1024]{1,0:T(8,128)S(1)}, f32[192,1024]{1,0:T(8,128)}, u32[]{:S(2)}) copy-start(f32[192,1024]{1,0:T(8,128)} %get-tuple-element.7) | copy-start | bytes 2359300
  205.9 2.1 copy-start.4
Sparse Core Ops, SparseCore 0:
  62.8 47.1 all-gather.2
  116.6 32.2 all-gather.4
  151.8 49.3 reduce-scatter.1
where the time goes:
time: 237 us
  blocking collectives  88.2 us (37%)
  waiting for transfers between devices  71.9 us (30%)
  starting transfers between devices  24.3 us (10%)
  matrix products  24.2 us (10%)
  between operations  13.9 us (6%)
  local copies, waits for them, and re-layouts  13.4 us (6%)
    all_to_all x1, blocking collectives, body(): lax.all_to_all(row_input, 'expert', split_axis=0, concat_axis=0, tiled=True)  49.3 us
    all_gather x1, waiting for transfers between devices, body(): inputs_all = lax.all_gather(flat_input, 'dp', axis=0, tiled=True)  38.1 us
    all_to_all x1, blocking collectives, body(): lax.all_to_all(out_blocks, 'dp', split_axis=0, concat_axis=3, tiled=True)  21.9 us
    all_to_all x1, waiting for transfers between devices, body(): lax.all_to_all(lax.all_to_all(out_blocks, 'dp', split_axis=0, concat_axis...  18.6 us
    all_to_all x1, starting transfers between devices, body(): lax.all_to_all(lax.all_to_all(out_blocks, 'dp', split_axis=0, concat_axis...  17.7 us
    all_to_all x1, blocking collectives, body(): lax.all_to_all(flat_cot, 'dp', split_axis=1, concat_axis=0, tiled=True)  17 us
    all_gather x1, waiting for transfers between devices, body(): hidden_all = lax.all_gather(hidden_part, 'dp', axis=0, tiled=True)  11.7 us
    all_to_all x1, starting transfers between devices, body(): lax.all_to_all(row_cot, 'expert', split_axis=0, concat_axis=0, tiled=True)  6.48 us
  transfers between devices with their start and end apart: 5, of which 4 were waited for; matrix products, arithmetic and copies ran while one was open for 13% of the time, Pallas kernels for 0%

commit v1 on v0

--- a/solution.py
+++ b/solution.py
@@ -50,7 +50,9 @@
         up_local, inputs_all, contract_last, preferred_element_type=jnp.float32
     )
     hidden_part = (jax.nn.silu(gate_pre) * up_pre).astype(jnp.bfloat16)
-    hidden_all = lax.all_gather(hidden_part, "dp", axis=0, tiled=True)
+    hidden_all = jnp.concatenate(
+        lax.all_to_all(jnp.stack([hidden_part] * lax.axis_size("dp")), "dp", 0, 0), axis=0
+    )
     contract_lead = (((0,), (0,)), ((), ()))
     expert_out = lax.dot_general(
         hidden_all, down_local, contract_lead, preferred_element_type=jnp.float32

time: 237 us -> 247 us (1.042)
  blocking collectives: 88.2 us -> 152 us
  waiting for transfers between devices: 71.9 us -> 22.1 us
  starting transfers between devices: 24.3 us -> 19.7 us
    all_to_all x0 -> x2, blocking collectives: none -> 70 us  [the longest x1 37.2 us: body(): lax.all_to_all(row_cot, 'expert', split_axis=0, concat_axis=0, tiled=True)]
    all_gather x1, waiting for transfers between devices: 38.1 us -> 0.02 us  [body(): inputs_all = lax.all_gather(flat_input, 'dp', axis=0, tiled=True)]
    all_gather x1 -> x0, waiting for transfers between devices: 11.7 us -> none  [body(): hidden_all = lax.all_gather(hidden_part, 'dp', axis=0, tiled=True)]
    all_to_all x1, blocking collectives: 21.9 us -> 14.9 us  [body(): lax.all_to_all(out_blocks, 'dp', split_axis=0, concat_axis=3, tiled=True)]
    all_to_all x1 -> x0, starting transfers between devices: 6.48 us -> none  [body(): lax.all_to_all(row_cot, 'expert', split_axis=0, concat_axis=0, tiled=True)]
    reduce_scatter x1, waiting for transfers between devices: 3.43 us -> 0.02 us  [body(): lax.psum_scatter(lax.dot_general(down_local, cot_quarter, contract_last,...]
    all_to_all x1, waiting for transfers between devices: 18.6 us -> 22 us  [body(): lax.all_to_all(lax.all_to_all(out_blocks, 'dp', split_axis=0, concat_axis...]
  transfers between devices with their start and end apart: 5 -> 3, of which waited for: 4 -> 1; matrix products, arithmetic and copies ran while one was open for 13% -> 11% of each run, Pallas kernels for 0% -> 0%
where the time goes in v1:
time: 247 us
  blocking collectives  152 us (62%)
  matrix products  22.7 us (9%)
  waiting for transfers between devices  22.1 us (9%)
  starting transfers between devices  19.7 us (8%)
  local copies, waits for them, and re-layouts  15 us (6%)
  between operations  14.3 us (6%)
    all_to_all x1, blocking collectives, body(): lax.all_to_all(row_input, 'expert', split_axis=0, concat_axis=0, tiled=True)  49.1 us
    all_to_all x1, blocking collectives, body(): lax.all_to_all(row_cot, 'expert', split_axis=0, concat_axis=0, tiled=True)  37.2 us
    all_to_all x1, blocking collectives, body(): lax.all_to_all(jnp.stack([hidden_part] * lax.axis_size('dp')), 'dp', 0, 0)  32.8 us
    all_to_all x1, waiting for transfers between devices, body(): lax.all_to_all(lax.all_to_all(out_blocks, 'dp', split_axis=0, concat_axis...  22 us
    all_to_all x1, starting transfers between devices, body(): lax.all_to_all(lax.all_to_all(out_blocks, 'dp', split_axis=0, concat_axis...  19.6 us
    all_to_all x1, blocking collectives, body(): lax.all_to_all(flat_cot, 'dp', split_axis=1, concat_axis=0, tiled=True)  18.4 us
    all_to_all x1, blocking collectives, body(): lax.all_to_all(out_blocks, 'dp', split_axis=0, concat_axis=3, tiled=True)  14.9 us
  transfers between devices with their start and end apart: 3, of which 1 were waited for; matrix products, arithmetic and copies ran while one was open for 11% of the time, Pallas kernels for 0%

profile of v1, /device:TPU:1, one launch (start us, length us, event | category | flops | bytes accessed | tf_op | source)
XLA Modules:
  0.0 246.8 jit_solution(8992099329016142953)
XLA Ops:
  7.2 0.0 copy-start
  7.2 0.0 all-gather.2.cloned.1.call-start
  7.2 0.8 copy.53
  8.0 0.1 convert_reduce_fusion
  8.2 0.8 copy.56
  9.0 0.1 select_reduce_fusion.1
  9.1 0.1 copy.54
  9.2 0.1 copy.57
  9.3 0.1 copy.55
  9.4 0.3 select_reduce_fusion
  9.7 0.1 copy.58
  9.8 1.3 convolution_convert_fusion
  11.1 1.1 copy.59
  12.2 49.1 %all_to_all.57 = bf16[128,2,2048]{2,1,0:T(2,128)(2,1)S(1)} all-to-all(bf16[128,2,2048]{2,1,0:T(2,128)(2,1)S(1)} %copy.59), channel_id=1, replica_groups=mesh['dp'=4,'expert'=128] {'expert'}, dimensions={0} | all-to-all | bytes 2097152 | tf_op jit(solution)/shard_map/all_to_all | solution.py:33
  61.3 1.2 reshape.96
  62.5 0.0 all-gather.2.cloned.1.call-update
  62.6 0.0 reduce-scatter.2.cloned.1.call-start
  62.6 0.1 copy.63
  62.7 0.5 fusion
  63.2 1.1 copy.65
  64.3 37.2 %all_to_all.58 = bf16[128,2,2048]{2,1,0:T(2,128)(2,1)S(1)} all-to-all(bf16[128,2,2048]{2,1,0:T(2,128)(2,1)S(1)} %copy.65), channel_id=1, replica_groups=mesh['dp'=4,'expert'=128] {'expert'}, dimensions={0} | all-to-all | bytes 2097152 | tf_op jit(solution)/shard_map/all_to_all | solution.py:34
  101.4 0.7 all_to_all.47
  102.1 0.2 copy.66
  102.3 18.4 %all_to_all.59 = bf16[256,4,512]{2,0,1:T(8,128)(2,1)S(1)} all-to-all(bf16[256,4,512]{2,0,1:T(8,128)(2,1)S(1)} %copy.66), channel_id=1, replica_groups=mesh['dp'=4,'expert'=128] {'dp'}, dimensions={1} | all-to-all | bytes 2097152 | tf_op jit(solution)/shard_map/all_to_all | solution.py:44
  120.8 2.7 %convolution_bitcast_fusion = f32[768,1024]{1,0:T(8,128)} fusion(bf16[1024,512]{1,0:T(8,128)(2,1)S(1)} %bitcast.60, bf16[1,768,512]{2,1,0:T(8,128)(2,1)S(1)} %copy-done), kind=kOutput, calls=%fused_computation.8 | convolution fusion | flops 805306368 | bytes 4980736 | tf_op jit(solution)/shard_map/dot_general | solution.py:64
  123.5 0.0 reduce-scatter.2.cloned.1.call-update
  123.5 0.0 all-gather.2.cloned.1.call-done
  123.5 1.1 copy-done.6
  124.6 3.9 %convolution_bitcast_fusion.2 = f32[192,1024]{1,0:T(8,128)S(1)} fusion(bf16[1024,2048]{1,0:T(8,128)(2,1)} %all-gather.2.cloned.1.call-done, bf16[1,192,2048]{2,1,0:T(8,128)(2,1)S(1)} %copy-done.6), kind=kOutput, calls=%fused_computation.13 | convolution fusion | flops 805306368 | bytes 5767168 | tf_op jit(solution)/shard_map/dot_general | solution.py:46
  128.5 2.5 %multiply_convert_fusion.2 = (bf16[192,1024]{1,0:T(8,128)(2,1)S(1)}, f32[192,1024]{1,0:T(8,128)}) fusion(f32[192,1024]{1,0:T(8,128)S(1)} %convolution_bitcast_fusion.2, bf16[1024,2048]{1,0:T(8,128)(2,1)S(1)} %copy-done.4, bf16[1,192,2048]{2,1,0:T(8,128)(2,1)S(1)} %copy-done.7), kind=kOutput, calls=%fused_computation.20 | convolution fusion | flops 806486016 | bytes 6946816 | tf_op jit(solution)/shard_map/dot_general | solution.py:49
  131.0 0.2 stack.2
  131.2 32.8 %all_to_all.60 = bf16[4,192,1024]{2,1,0:T(8,128)(2,1)S(1)} all-to-all(bf16[4,192,1024]{2,1,0:T(8,128)(2,1)S(1)} %stack.2), channel_id=1, replica_groups=mesh['dp'=4,'expert'=128] {'dp'}, dimensions={0} | all-to-all | bytes 3145728 | tf_op jit(solution)/shard_map/all_to_all | solution.py:54
  164.0 1.2 copy-done.1
  165.3 2.0 convolution_convert_fusion.4
  167.3 1.5 reshape.98
  168.7 2.0 copy.60
  170.8 14.9 %all_to_all.61 = bf16[4,128,2,512]{1,3,2,0:T(8,128)(2,1)S(1)} all-to-all(bf16[4,128,2,512]{1,3,2,0:T(8,128)(2,1)} %copy.60), channel_id=1, replica_groups=mesh['dp'=4,'expert'=128] {'dp'}, dimensions={0} | all-to-all | bytes 2097152 | tf_op jit(solution)/shard_map/all_to_all | solution.py:82
  185.7 0.1 copy.61
  185.8 2.1 copy.62
  187.8 19.6 %all-to-all-start.3 = ((bf16[1,128,2,2048]{3,2,0,1:T(2,128)(2,1)}), bf16[1,128,2,2048]{3,2,0,1:T(2,128)(2,1)S(1)}, u32[]{:S(2)}, u32[]{:S(2)}) async-start(bf16[1,128,2,2048]{3,2,0,1:T(2,128)(2,1)} %copy.62), calls=%async_computation.3 | async-start | bytes 2097152 | tf_op jit(solution)/shard_map/all_to_all | solution.py:81
  207.5 0.2 broadcast_select_fusion
  207.7 0.0 reduce-scatter.2.cloned.1.call-done
  207.7 4.7 %fusion.2 = bf16[1,192,2048]{2,1,0:T(8,128)(2,1)} fusion(bf16[1024,2048]{1,0:T(8,128)(2,1)} %all-gather.2.cloned.1.call-done, f32[192,1024]{1,0:T(8,128)} %reduce-scatter.2.cloned.1.call-done, f32[192,1024]{1,0:T(8,128)} %copy-done.9), kind=kOutput, calls=%fused_computation.6 | convolution fusion | flops 806879232 | bytes 6553600 | tf_op jit(solution)/shard_map/dot_general | solution.py:77
  212.5 2.0 fusion.1
  214.5 1.9 fusion.3
  216.4 22.0 %all-to-all-done.3 = bf16[1,128,2,2048]{3,2,0,1:T(2,128)(2,1)S(1)} async-done(((bf16[1,128,2,2048]{3,2,0,1:T(2,128)(2,1)}), bf16[1,128,2,2048]{3,2,0,1:T(2,128)(2,1)S(1)}, u32[]{:S(2)}, u32[]{:S(2)}) %all-to-all-start.3) | async-done | bytes 1048608 | tf_op jit(solution)/shard_map/all_to_all | solution.py:81
  238.4 0.4 reshape.99
  238.8 1.2 convolution_convert_fusion.3
  (24 shorter events, 0.1 us)
Async XLA Ops:
  7.2 113.6 %copy-start = (bf16[1,768,512]{2,1,0:T(8,128)(2,1)S(1)}, bf16[1,768,512]{2,1,0:T(8,128)(2,1)}, u32[]{:S(2)}) copy-start(bf16[1,768,512]{2,1,0:T(8,128)(2,1)} %param.13) | copy-start | bytes 2359300
  7.2 116.4 %all-gather.2.cloned.1.call-start = ((), (), s32[]{:S(2)}) async-start(), calls=%async_computation.7 | async-start | bytes 5242880 | tf_op jit(solution)/shard_map/all_gather | solution.py:43
  61.3 1.4 copy-start.3
  62.6 145.1 %reduce-scatter.2.cloned.1.call-start = ((), (), s32[]{:S(2)}) async-start(), calls=%async_computation.8 | async-start | bytes 3932160 | tf_op jit(solution)/shard_map/reduce_scatter | solution.py:63
  123.5 1.1 copy-start.6
  123.5 5.0 %copy-start.7 = (bf16[1,192,2048]{2,1,0:T(8,128)(2,1)S(1)}, bf16[1,192,2048]{2,1,0:T(8,128)(2,1)}, u32[]{:S(2)}) copy-start(bf16[1,192,2048]{2,1,0:T(8,128)(2,1)} %param.12) | copy-start | bytes 2359300
  124.6 3.9 %copy-start.4 = (bf16[1024,2048]{1,0:T(8,128)(2,1)S(1)}, bf16[1024,2048]{1,0:T(8,128)(2,1)}, u32[]{:S(2)}) copy-start(bf16[1024,2048]{1,0:T(8,128)(2,1)} %all-gather.2.cloned.1.call-done) | copy-start | bytes 12582916
  128.5 2.5 %copy-start.9 = (f32[192,1024]{1,0:T(8,128)}, f32[192,1024]{1,0:T(8,128)S(1)}, u32[]{:S(2)}) copy-start(f32[192,1024]{1,0:T(8,128)S(1)} %convolution_bitcast_fusion.2) | copy-start | bytes 2359300
  164.0 1.2 copy-start.1
  187.8 50.5 %all-to-all-start.3 = ((bf16[1,128,2,2048]{3,2,0,1:T(2,128)(2,1)}), bf16[1,128,2,2048]{3,2,0,1:T(2,128)(2,1)S(1)}, u32[]{:S(2)}, u32[]{:S(2)}) async-start(bf16[1,128,2,2048]{3,2,0,1:T(2,128)(2,1)} %copy.62), calls=%async_computation.3 | async-start | bytes 2097152 | tf_op jit(solution)/shard_map/all_to_all | solution.py:81
  207.7 4.8 %copy-start.5 = (bf16[1024,2048]{1,0:T(8,128)(2,1)S(1)}, bf16[1024,2048]{1,0:T(8,128)(2,1)}, u32[]{:S(2)}) copy-start(bf16[1024,2048]{1,0:T(8,128)(2,1)} %all-gather.2.cloned.1.call-done) | copy-start | bytes 12582916
  207.7 4.8 %copy-start.8 = (f32[192,1024]{1,0:T(8,128)S(1)}, f32[192,1024]{1,0:T(8,128)}, u32[]{:S(2)}) copy-start(f32[192,1024]{1,0:T(8,128)} %reduce-scatter.2.cloned.1.call-done) | copy-start | bytes 2359300
  207.7 4.7 %copy-start.10 = (f32[192,1024]{1,0:T(8,128)S(1)}, f32[192,1024]{1,0:T(8,128)}, u32[]{:S(2)}) copy-start(f32[192,1024]{1,0:T(8,128)} %copy-done.9) | copy-start | bytes 2359300
  207.7 4.7 %copy-start.11 = (f32[192,1024]{1,0:T(8,128)S(1)}, f32[192,1024]{1,0:T(8,128)}, u32[]{:S(2)}) copy-start(f32[192,1024]{1,0:T(8,128)} %get-tuple-element.7) | copy-start | bytes 2359300
  212.5 2.0 copy-start.2
Sparse Core Ops, SparseCore 0:
  62.7 47.1 all-gather.1
  123.6 58.5 reduce-scatter.1
